TPU v7x, 512 devices: a whole 4x4x16 slice. The times are simulated.
512 devices in a mesh: tm: 4 (over y), prefix: 128 (over x, z, core).
Axes of the slice: x: 4, y: 4, z: 16, core: 2. Of those that a mesh axis runs over, the one named last changes fastest.
Arguments:
- traffic: bfloat16 [262144, 4096], P('prefix', 'tm'), as said below
- start_level: float32 [262144], P('prefix'), as said below
- subspace: bfloat16 [262144, 64], P('prefix'), as said below
Outputs:
- scores: float32 [64, 4096], P(None, 'tm')
- energy: float32 [4096], P('tm')
Inputs may be any that keep to these rules, and one draw needn't show every extreme that they name: `traffic`: traffic volumes of one prefix pair per bin; each series keeps one typical level across all bins. `start_level`: each series' starting level lies within a factor of two of its typical traffic. `subspace`: each column has about unit length.
All inputs are finite; a program needn't handle non-finite values.
Results may differ from a plain program's by a relative error of at most 0.003.
Values sent between devices are 32-bit elements; how exact they have to be, the bound alone decides.
No kernel may reach another device: no remote copies, remote signals or barrier semaphores. Data moves between devices by JAX's collectives and lax.ppermute only.
A program may use at most 64 MiB of HBM per device.

v0:
```python
import math
import jax
import jax.numpy as jnp
from jax import lax
from jax.sharding import PartitionSpec as P

BLOCK = 256
ewma_rate = 0.002


def entering(x, axis, combine, identity):
    count, place = (lax.axis_size(axis), lax.axis_index(axis))
    everything = jax.tree.map(lambda part: lax.all_gather(part, axis), x)
    start = jax.tree.map(
        lambda part, zero: jnp.broadcast_to(jnp.asarray(zero, part.dtype), part.shape), x, identity
    )

    def lap(k, before):
        reached = k < place
        new = combine(before, jax.tree.map(lambda part: part[k], everything))
        return jax.tree.map(lambda a, b: jnp.where(reached, a, b), new, before)

    return lax.fori_loop(0, count, lap, start)


def combine(earlier, later):
    return (earlier[0] * later[0], later[0] * earlier[1] + later[1])


def shards(traffic, start_level, subspace):
    series, width = traffic.shape
    count_blocks = width // BLOCK
    keep_rate = 1.0 - ewma_rate
    log_keep = math.log(keep_rate)
    offsets = jnp.arange(BLOCK)
    lag_matrix = (offsets[None, :] - offsets[:, None] - 1).astype(jnp.float32)
    strict_qp = jnp.where(
        lag_matrix >= 0.0,
        (ewma_rate * keep_rate ** jnp.maximum(lag_matrix, 0.0)).astype(jnp.bfloat16),
        jnp.zeros((), jnp.bfloat16),
    )
    tail_lags = (BLOCK - 1 - offsets).astype(jnp.float32)
    tail_weights = (ewma_rate * keep_rate**tail_lags).astype(jnp.bfloat16)
    flat_blocks = traffic.reshape(series * count_blocks, BLOCK)
    inner_sum = jnp.dot(flat_blocks, strict_qp, preferred_element_type=jnp.float32)
    block_ends = jnp.dot(flat_blocks, tail_weights, preferred_element_type=jnp.float32).reshape(
        series, count_blocks
    )
    block_ids = jnp.arange(count_blocks).astype(jnp.float32)
    block_gap = block_ids[:, None] - block_ids[None, :] - 1.0
    carry_mix = jnp.where(
        block_gap >= 0, jnp.exp(BLOCK * jnp.maximum(block_gap, 0.0) * log_keep), 0.0
    )
    local_entry = jnp.dot(block_ends, carry_mix.T, precision=lax.Precision.HIGHEST)
    closing_weights = jnp.exp(BLOCK * (count_blocks - 1.0 - block_ids) * log_keep)
    local_close = jnp.dot(block_ends, closing_weights, precision=lax.Precision.HIGHEST)
    factor = jnp.full((1,), math.exp(width * log_keep), jnp.float32)
    identity = (jnp.ones((1,), jnp.float32), jnp.zeros((series,), jnp.float32))
    prefix_factor, prefix_value = entering((factor, local_close), "tm", combine, identity)
    carry_entry = prefix_factor * start_level + prefix_value
    level_entry = (
        local_entry + jnp.exp(BLOCK * block_ids * log_keep)[None, :] * carry_entry[:, None]
    )
    step_powers = jnp.exp(offsets.astype(jnp.float32) * log_keep)
    previous = inner_sum + step_powers[None, :] * level_entry.reshape(series * count_blocks, 1)
    residual = (
        (flat_blocks.astype(jnp.float32) - previous).astype(jnp.bfloat16).reshape(series, width)
    )
    local_scores = lax.dot_general(
        subspace, residual, (((0,), (0,)), ((), ())), preferred_element_type=jnp.float32
    )
    series_total = series * lax.axis_size("prefix")
    scores = lax.psum(local_scores, "prefix")
    scores_low = scores.astype(jnp.bfloat16)
    normal_part = jnp.dot(subspace, scores_low, preferred_element_type=jnp.float32)
    remainder = residual.astype(jnp.float32) - normal_part
    energy = lax.psum(jnp.sum(remainder * remainder, axis=0), "prefix") / series_total
    return (scores, energy)


def solution(mesh):
    return jax.shard_map(
        shards,
        mesh=mesh,
        in_specs=(P("prefix", "tm"), P("prefix"), P("prefix", None)),
        out_specs=(P(None, "tm"), P("tm")),
        check_vma=False,
    )
```

profile of v0, /device:TPU:1, one launch (start us, length us, event | category | flops | bytes accessed | tf_op | source)
XLA Modules:
  0.0 704.0 jit_solution(9338106033665262471)
XLA Ops:
  7.3 7.8 %dot_general.28 = bf16[2048,4,256]{2,1,0:T(4,128)(2,1)} reshape(bf16[2048,1024]{1,0:T(8,128)(2,1)} %param.5) | data formatting | bytes 8388608 | tf_op jit(solution)/shard_map/dot_general | solution.py:46
  15.1 7.5 %reshape.38 = bf16[8192,256]{1,0:T(8,128)(2,1)} reshape(bf16[2048,1024]{1,0:T(8,128)(2,1)} %param.5) | data formatting | bytes 8388608 | tf_op jit(solution)/shard_map/reshape | solution.py:44
  22.7 22.6 %multiply_reduce_fusion = f32[2048,4]{1,0:T(8,128)S(1)} fusion(f32[256]{0:T(256)S(1)} %fusion.24, bf16[2048,4,256]{2,1,0:T(4,128)(2,1)} %dot_general.28), kind=kLoop, calls=%fused_computation.10 | loop fusion | flops 6283264 | bytes 4228096 | tf_op jit(solution)/shard_map/dot_general | solution.py:46
  45.3 1.0 fusion.25
  46.3 10.4 %all-gather = f32[8192]{0:T(1024)S(1)} all-gather(f32[2048]{0:T(1024)S(1)} %bitcast.44), channel_id=2, replica_groups=mesh['tm'=4,'prefix'=128] {'tm'}, dimensions={0}, use_global_device_ids=true | all-gather | bytes 40960 | tf_op jit(solution)/shard_map/all_gather | solution.py:13
  56.7 1.3 dynamic-slice
  57.9 0.8 dynamic-update-slice
  58.7 8.4 %all-reduce = f32[4]{0:T(128)S(1)} all-reduce(f32[4]{0:T(128)S(1)} %dynamic-update-slice), channel_id=1, replica_groups=mesh['tm'=4,'prefix'=128] {'tm'}, use_global_device_ids=true, to_apply=%add | all-reduce | flops 4 | bytes 32
  67.1 8.4 %while.16 = (s32[]{:T(128)}, f32[1]{0:T(128)}, f32[2048]{0:T(1024)S(1)}, s32[]{:T(128)}, f32[4,1]{0,1:T(1,128)S(1)}, /*index=5*/f32[4,2048]{1,0:T(4,128)S(1)}, s32[]{:T(128)}, s32[]{:T(128)}) while((s32[]{:T(128)}, f32[1]{0:T(128)}, f32[2048]{0:T(1024)S(1)}, s32[]{:T(128)}, f32[4,1]{0,1:T(1,128)S(1)}, ...), condition=%wide.region_1.2_spmd.clone, body=%wide.region_0.1_spmd.clone.sunk | while | flops 8198 | bytes 41110 | solution.py:23
  67.8 0.7 add_select_fusion.2
  69.9 0.7 add_select_fusion.2
  72.0 0.7 add_select_fusion.2
  74.0 0.7 add_select_fusion.2
  75.5 1.0 convolution_add_fusion
  77.5 6.3 copy.9
  83.9 8.0 %fusion.2 = bf16[8192,256]{0,1:T(8,128)(2,1)} fusion(bf16[8192,256]{1,0:T(8,128)(2,1)} %reshape.38, bf16[8192,256]{0,1:T(8,128)(2,1)} %copy.9, f32[8192]{0:T(1024)S(1)} %mul.132, f32[256]{0:T(256)S(1)} %multiply_exponential_fusion), kind=kOutput, calls=%fused_computation.6 | convolution fusion | flops 1084751872 | bytes 12616704 | tf_op jit(solution)/shard_map/dot_general | solution.py:45
  91.9 6.4 copy.11
  98.3 7.5 %reshape.39 = bf16[2048,1024]{1,0:T(8,128)(2,1)} reshape(bf16[8192,256]{1,0:T(8,128)(2,1)} %copy.11) | data formatting | bytes 8388608 | tf_op jit(solution)/shard_map/reshape | solution.py:67
  105.8 3.7 convolution_bitcast_fusion.1
  109.6 6.5 copy.12
  116.1 328.3 %all-reduce.3.cloned.1.call-done = f32[64,1024]{1,0:T(8,128)} async-done(((f32[64,1024]{1,0:T(8,128)}), f32[64,1024]{1,0:T(8,128)}) %all-reduce.3.cloned.1.call-update) | async-done | bytes 262160 | tf_op jit(solution)/shard_map/psum | solution.py:73
  444.4 3.7 fusion.4
  448.2 247.7 %psum.15 = f32[1024]{0:T(1024)S(1)} all-reduce(f32[1024]{0:T(1024)S(1)} %fusion.4), channel_id=1, replica_groups=mesh['tm'=4,'prefix'=128] {'prefix'}, use_global_device_ids=true, to_apply=%region_4.5 | all-reduce | flops 1024 | bytes 8192 | tf_op jit(solution)/shard_map/psum | solution.py:77
  696.5 0.7 copy.30
  (27 shorter events, 4.4 us)
Async XLA Ops:
  7.2 98.6 %copy-start = (bf16[2048,64]{0,1:T(8,128)(2,1)S(1)}, bf16[2048,64]{0,1:T(8,128)(2,1)}, u32[]{:S(2)}) copy-start(bf16[2048,64]{0,1:T(8,128)(2,1)} %param.7) | copy-start | bytes 786436
  7.2 437.3 %all-reduce.3.cloned.1.call-start = ((), (), s32[]{:S(2)}) async-start(), calls=%async_computation | async-start | bytes 524288 | tf_op jit(solution)/shard_map/psum | solution.py:73
  22.7 52.8 %copy-start.2 = (f32[2048]{0:T(1024)S(1)}, f32[2048]{0:T(1024)}, u32[]{:S(2)}) copy-start(f32[2048]{0:T(1024)} %param.6) | copy-start | bytes 24580
  444.4 252.0 %copy-start.1 = (f32[64,1024]{1,0:T(8,128)S(1)}, f32[64,1024]{1,0:T(8,128)}, u32[]{:S(2)}) copy-start(f32[64,1024]{1,0:T(8,128)} %all-reduce.3.cloned.1.call-done) | copy-start | bytes 786436
Sparse Core Ops, SparseCore 0:
  109.7 334.7 all-reduce.2
where the time goes:
time: 705 us; the launch traced here: 704 us
  waiting for transfers between devices  328 us (47%)
  blocking collectives  266 us (38%)
  local copies, waits for them, and re-layouts  48.7 us (7%)
  other arithmetic  26 us (4%)
  matrix products  17.5 us (2%)
  between operations  14.1 us (2%)
    psum x1, waiting for transfers between devices, shards(): scores = lax.psum(local_scores, 'prefix')  328 us
    psum x1, blocking collectives, shards(): lax.psum(jnp.sum(remainder * remainder, axis=0), 'prefix') / series_total  248 us
    dot_general x1, other arithmetic, shards(): jnp.dot(flat_blocks, tail_weights, preferred_element_type=jnp.float32)  22.6 us
  transfers between devices with their start and end apart: 1, of which 1 were waited for; matrix products, arithmetic and copies ran while one was open for 1% of the time, Pallas kernels for 0%

commit v1 on v0

--- a/solution.py
+++ b/solution.py
@@ -70,7 +70,7 @@
         subspace, residual, (((0,), (0,)), ((), ())), preferred_element_type=jnp.float32
     )
     series_total = series * lax.axis_size("prefix")
-    scores = lax.psum(local_scores, "prefix")
+    scores = jnp.sum(lax.all_gather(local_scores, "prefix"), axis=0)
     scores_low = scores.astype(jnp.bfloat16)
     normal_part = jnp.dot(subspace, scores_low, preferred_element_type=jnp.float32)
     remainder = residual.astype(jnp.float32) - normal_part

time: 705 us -> 584 us (0.83)
  waiting for transfers between devices: 328 us -> 197 us
  other arithmetic: 26 us -> 37.6 us
    psum x1 -> x0, waiting for transfers between devices: 328 us -> none  [shards(): scores = lax.psum(local_scores, 'prefix')]
    all_gather x0 -> x1, waiting for transfers between devices: none -> 197 us  [shards(): scores = jnp.sum(lax.all_gather(local_scores, 'prefix'), axis=0)]
    reduce_sum x0 -> x1, other arithmetic: none -> 11.9 us  [shards(): scores = jnp.sum(lax.all_gather(local_scores, 'prefix'), axis=0)]
where the time goes in v1:
time: 584 us; the launch traced here: 582 us
  blocking collectives  265 us (45%)
  waiting for transfers between devices  197 us (34%)
  local copies, waits for them, and re-layouts  47.8 us (8%)
  other arithmetic  37.6 us (6%)
  matrix products  17.5 us (3%)
  between operations  14.1 us (2%)
    psum x1, blocking collectives, shards(): lax.psum(jnp.sum(remainder * remainder, axis=0), 'prefix') / series_total  246 us
    all_gather x1, waiting for transfers between devices, shards(): scores = jnp.sum(lax.all_gather(local_scores, 'prefix'), axis=0)  197 us
    dot_general x1, other arithmetic, shards(): jnp.dot(flat_blocks, tail_weights, preferred_element_type=jnp.float32)  22.6 us
    reshape x2, local copies, waits for them, and re-layouts, shards(): (flat_blocks.astype(jnp.float32) - previous).astype(jnp.bfloat16)  14 us
    reshape x2, local copies, waits for them, and re-layouts, shards(): flat_blocks = traffic.reshape(series * count_blocks, BLOCK)  13.9 us
    reduce_sum x1, other arithmetic, shards(): scores = jnp.sum(lax.all_gather(local_scores, 'prefix'), axis=0)  11.9 us
  transfers between devices with their start and end apart: 1, of which 1 were waited for; matrix products, arithmetic and copies ran while one was open for 1% of the time, Pallas kernels for 0%

profile of v1, /device:TPU:1, one launch (start us, length us, event | category | flops | bytes accessed | tf_op | source)
XLA Modules:
  0.0 581.7 jit_solution(5940654040581678776)
XLA Ops:
  7.3 7.5 %reshape.38 = bf16[8192,256]{1,0:T(8,128)(2,1)} reshape(bf16[2048,1024]{1,0:T(8,128)(2,1)} %param.5) | data formatting | bytes 8388608 | tf_op jit(solution)/shard_map/reshape | solution.py:44
  14.8 7.9 %dot_general.28 = bf16[2048,4,256]{2,1,0:T(4,128)(2,1)} reshape(bf16[2048,1024]{1,0:T(8,128)(2,1)} %param.5) | data formatting | bytes 8388608 | tf_op jit(solution)/shard_map/dot_general | solution.py:46
  22.7 1.3 dynamic-slice
  24.0 0.8 dynamic-update-slice
  24.8 9.5 %all-reduce = f32[4]{0:T(128)S(1)} all-reduce(f32[4]{0:T(128)S(1)} %dynamic-update-slice), channel_id=1, replica_groups=mesh['tm'=4,'prefix'=128] {'tm'}, use_global_device_ids=true, to_apply=%add | all-reduce | flops 4 | bytes 32
  34.3 6.4 %copy.9 = bf16[8192,256]{0,1:T(8,128)(2,1)} copy(bf16[8192,256]{1,0:T(8,128)(2,1)} %reshape.38) | data formatting | bytes 8388608 | tf_op jit(solution)/shard_map/reshape | solution.py:44
  40.7 22.6 %multiply_reduce_fusion = f32[2048,4]{1,0:T(8,128)S(1)} fusion(f32[256]{0:T(256)S(1)} %fusion.24, bf16[2048,4,256]{2,1,0:T(4,128)(2,1)} %dot_general.28), kind=kLoop, calls=%fused_computation.10 | loop fusion | flops 6283264 | bytes 4228096 | tf_op jit(solution)/shard_map/dot_general | solution.py:46
  63.3 1.0 fusion.25
  64.3 9.2 %all-gather = f32[8192]{0:T(1024)S(1)} all-gather(f32[2048]{0:T(1024)S(1)} %bitcast.46), channel_id=2, replica_groups=mesh['tm'=4,'prefix'=128] {'tm'}, dimensions={0}, use_global_device_ids=true | all-gather | bytes 40960 | tf_op jit(solution)/shard_map/all_gather | solution.py:13
  73.5 7.7 %while.16 = (s32[]{:T(128)}, f32[1]{0:T(128)}, f32[2048]{0:T(1024)S(1)}, s32[]{:T(128)}, f32[4,1]{0,1:T(1,128)S(1)}, /*index=5*/f32[4,2048]{1,0:T(4,128)S(1)}, s32[]{:T(128)}, s32[]{:T(128)}) while((s32[]{:T(128)}, f32[1]{0:T(128)}, f32[2048]{0:T(1024)S(1)}, s32[]{:T(128)}, f32[4,1]{0,1:T(1,128)S(1)}, ...), condition=%wide.region_1.2_spmd.clone, body=%wide.region_0.1_spmd.clone.sunk | while | flops 8198 | bytes 41118 | solution.py:23
  74.8 0.6 add_select_fusion.2
  76.7 0.6 add_select_fusion.2
  78.6 0.6 add_select_fusion.2
  81.2 1.0 convolution_add_fusion
  82.6 0.6 mul.132
  83.2 8.0 %fusion.2 = bf16[8192,256]{0,1:T(8,128)(2,1)} fusion(bf16[8192,256]{1,0:T(8,128)(2,1)} %reshape.38, bf16[8192,256]{0,1:T(8,128)(2,1)} %copy.9, f32[8192]{0:T(1024)S(1)} %mul.132, f32[256]{0:T(256)S(1)} %multiply_exponential_fusion), kind=kOutput, calls=%fused_computation.6 | convolution fusion | flops 1084751872 | bytes 12616704 | tf_op jit(solution)/shard_map/dot_general | solution.py:45
  91.3 6.4 %copy.11 = bf16[8192,256]{1,0:T(8,128)(2,1)} copy(bf16[8192,256]{0,1:T(8,128)(2,1)} %fusion.2) | data formatting | bytes 8388608 | tf_op jit(solution)/shard_map/convert_element_type | solution.py:67
  97.6 7.5 %reshape.39 = bf16[2048,1024]{1,0:T(8,128)(2,1)} reshape(bf16[8192,256]{1,0:T(8,128)(2,1)} %copy.11) | data formatting | bytes 8388608 | tf_op jit(solution)/shard_map/reshape | solution.py:67
  105.2 3.7 convolution_bitcast_fusion.1
  108.9 6.5 %copy.12 = bf16[2048,1024]{0,1:T(8,128)(2,1)} copy(bf16[2048,1024]{1,0:T(8,128)(2,1)} %reshape.39) | data formatting | bytes 8388608 | tf_op jit(solution)/shard_map/reshape | solution.py:67
  115.5 196.9 %all-gather.4.cloned.1.call-done = f32[8192,1024]{1,0:T(8,128)} async-done(((f32[64,1024]{1,0:T(8,128)}), f32[8192,1024]{1,0:T(8,128)}) %all-gather.4.cloned.1.call-update) | async-done | bytes 33554448 | tf_op jit(solution)/shard_map/all_gather | solution.py:73
  312.3 11.9 %reduce_sum.18 = f32[64,1024]{1,0:T(8,128)S(1)} reduce(f32[128,64,1024]{2,1,0:T(8,128)} %bitcast.44, f32[]{:T(128)} %constant.30.clone.1), dimensions={0}, to_apply=%region_2.3 | reduce | flops 8323072 | bytes 33816580 | tf_op jit(solution)/shard_map/reduce_sum | solution.py:73
  324.2 3.7 fusion.4
  327.9 246.4 %psum.7 = f32[1024]{0:T(1024)S(1)} all-reduce(f32[1024]{0:T(1024)S(1)} %fusion.4), channel_id=1, replica_groups=mesh['tm'=4,'prefix'=128] {'prefix'}, use_global_device_ids=true, to_apply=%region_4.5 | all-reduce | flops 1024 | bytes 8192 | tf_op jit(solution)/shard_map/psum | solution.py:77
  (27 shorter events, 4.2 us)
Async XLA Ops:
  7.2 98.0 %copy-start = (bf16[2048,64]{0,1:T(8,128)(2,1)S(1)}, bf16[2048,64]{0,1:T(8,128)(2,1)}, u32[]{:S(2)}) copy-start(bf16[2048,64]{0,1:T(8,128)(2,1)} %param.7) | copy-start | bytes 786436
  7.2 305.1 %all-gather.4.cloned.1.call-start = ((), (), s32[]{:S(2)}) async-start(), calls=%async_computation | async-start | bytes 33816576 | tf_op jit(solution)/shard_map/all_gather | solution.py:73
  40.7 40.5 %copy-start.2 = (f32[2048]{0:T(1024)S(1)}, f32[2048]{0:T(1024)}, u32[]{:S(2)}) copy-start(f32[2048]{0:T(1024)} %param.6) | copy-start | bytes 24580
  324.2 250.7 %copy-start.1 = (f32[64,1024]{1,0:T(8,128)}, f32[64,1024]{1,0:T(8,128)S(1)}, u32[]{:S(2)}) copy-start(f32[64,1024]{1,0:T(8,128)S(1)} %reduce_sum.18) | copy-start | bytes 786436
Sparse Core Ops, SparseCore 0:
  109.1 203.1 all-gather.3
